TPU v7x, 32 devices: a whole 2x2x4 slice. The times are simulated.
32 devices in a mesh: mode: 8 (over z, y), tm: 4 (over x, core).
Axes of the slice: x: 2, y: 2, z: 4, core: 2. Of those that a mesh axis runs over, the one named last changes fastest.
Arguments:
- support_accel: bfloat16 [512, 2048], P(None, 'tm'), may hold values from -6 to 6
- participation: bfloat16 [2048, 512], P('mode'), may hold values from -0.25 to 0.25
- kernels: float32 [2048, 2048], P('mode'), may hold values from -0.25 to 0.25
- lengths: int32 [2048], P('mode'), may hold values from 1 to 2048, as said below
- mode_shapes: bfloat16 [16384, 2048], P('mode'), may hold values from -0.125 to 0.125
- groups: int32 [16384], P('mode'), may hold values from 0 to 511
Outputs:
- response: bfloat16 [16384, 2048], P('mode', 'tm')
Inputs may be any that keep to these rules, and one draw needn't show every extreme that they name: `lengths`: some mode has exactly 2048 taps in every draw.
All inputs are finite; a program needn't handle non-finite values.
Results may differ from a plain program's by a relative error of at most 0.0033.
Values may be sent and summed in bfloat16 or wider, within the bound.
A program may use at most 64 MiB of HBM per device.

v0:
```python
import jax
import jax.numpy as jnp
from jax import lax
from jax.sharding import PartitionSpec as P


def passed_along(block, axis, distance):
    devices = range(lax.axis_size(axis))
    route = [(i - distance, i) for i in devices if i - distance in devices]
    return lax.ppermute(block, axis, route)


def depthwise(signal, weights):
    flipped = jnp.flip(weights, 1)[:, None, :]
    result = lax.conv_general_dilated(
        signal[None],
        flipped,
        (1,),
        "VALID",
        dimension_numbers=("NCH", "OIH", "NCH"),
        feature_group_count=signal.shape[0],
        precision=lax.Precision.HIGHEST,
    )
    return result[0]


def apply_filter(signal, kernel):
    return depthwise(signal, kernel)


def per_device(support_accel, participation, kernels, lengths, mode_shapes, groups):
    slab_len = support_accel.shape[1]
    tap_count = kernels.shape[1]
    depth_slabs = tap_count // slab_len
    forces = jnp.dot(participation, support_accel, preferred_element_type=jnp.float32)
    alive = jnp.arange(tap_count, dtype=jnp.int32)[None, :] < lengths[:, None]
    masked = jnp.where(alive, kernels, jnp.zeros_like(kernels))
    pieces = [forces]
    for distance in range(1, depth_slabs + 1):
        pieces.insert(0, passed_along(forces, "tm", distance))
    window = jnp.concatenate(pieces, axis=1)
    modal = apply_filter(window[:, 1:], masked).astype(jnp.bfloat16)
    initial = jnp.zeros((mode_shapes.shape[0], slab_len), jnp.float32)
    piece = jax.tree.map(lambda part: lax.all_gather(part, "mode", axis=0, tiled=True), modal)
    columns = lax.slice_in_dim(mode_shapes, 0, piece.shape[0], axis=1)
    summed = initial + jnp.dot(columns, piece, preferred_element_type=jnp.float32)
    ground = jnp.take(support_accel, groups, axis=0).astype(jnp.float32)
    return (summed + ground).astype(jnp.bfloat16)


def solution(mesh):
    placed = (
        P(None, "tm"),
        P("mode", None),
        P("mode", None),
        P("mode"),
        P("mode", None),
        P("mode"),
    )
    return jax.shard_map(
        per_device, mesh=mesh, in_specs=placed, out_specs=P("mode", "tm"), check_vma=False
    )
```

profile of v0, /device:TPU:0, one launch (start us, length us, event | category | flops | bytes accessed | tf_op | source)
XLA Modules:
  0.0 271.4 jit_solution(18268262673586640301)
XLA Ops:
  6.5 0.0 copy-start
  6.5 0.0 all-gather.3.cloned.1.call-start
  6.5 1.0 copy-done
  7.6 1.2 fusion.4
  8.8 1.5 collective-permute-start
  10.3 5.1 %collective-permute-start.1 = (f32[256,512]{1,0:T(8,128)S(1)}, f32[256,512]{1,0:T(8,128)}, u32[]{:S(2)}, u32[]{:S(2)}) collective-permute-start(f32[256,512]{1,0:T(8,128)S(1)} %fusion.4), channel_id=1, source_target_pairs={{0,3},{4,7},{8,11},{12,15},{16,19},{20,23},{24,27},{28,31}} | collective-permute-start | bytes 1572872 | tf_op jit(solution)/shard_map/ppermute | solution.py:10
  15.4 2.1 collective-permute-start.2
  17.5 2.1 collective-permute-start.3
  19.6 1.8 fusion.2
  21.4 11.6 %rev.4 = f32[256,2048]{1,0:T(8,128)} reverse(f32[256,2048]{1,0:T(8,128)S(1)} %fusion.2), dimensions={1} | reverse | bytes 4194304 | tf_op jit(solution)/shard_map/jit(_flip)/rev | solution.py:14
  33.0 6.1 %copy.12 = f32[256,1,2048]{0,1,2:T(1,128)} copy(f32[256,1,2048]{2,0,1:T(8,128)} %bitcast.15) | data formatting | bytes 4194304 | tf_op jit(solution)/shard_map/broadcast_in_dim | solution.py:14
  39.1 0.0 collective-permute-done
  39.1 1.1 constant_dynamic-update-slice_fusion.4
  40.2 0.0 collective-permute-done.1
  40.2 1.1 constant_dynamic-update-slice_fusion.3
  41.3 0.0 collective-permute-done.2
  41.3 1.1 constant_dynamic-update-slice_fusion.2
  42.3 0.0 collective-permute-done.3
  42.4 1.1 constant_dynamic-update-slice_fusion.1
  43.5 0.8 slice_bitcast_fusion
  44.2 4.0 %copy.11 = f32[1,256,2559]{1,0,2:T(1,128)} copy(f32[1,256,2559]{2,1,0:T(8,128)S(1)} %slice_bitcast_fusion) | data formatting | bytes 5240832 | tf_op jit(solution)/shard_map/broadcast_in_dim | solution.py:16
  48.3 0.0 copy-start.1
  48.3 90.9 %convolution_convert_fusion = bf16[1,256,512]{1,0,2:T(2,128)(2,1)} fusion(f32[1,256,2559]{1,0,2:T(1,128)} %copy.11, f32[256,1,2048]{0,1,2:T(1,128)} %copy.12), kind=kOutput, calls=%fused_computation.7 | convolution fusion | flops 3221356544 | bytes 4979712 | tf_op jit(solution)/shard_map/conv_general_dilated | solution.py:15
  139.1 0.0 all-gather.3.cloned.1.call-update
  139.2 0.0 copy-done.1
  139.2 7.5 %gather_fusion = bf16[2048,512]{1,0:T(8,128)(2,1)S(1)} fusion(bf16[512,512]{1,0:T(8,128)(2,1)S(1)} %copy-done, s32[2048]{0:T(1024)S(1)} %fusion.3), kind=kCustom, calls=%fused_computation | custom fusion | bytes 4202496 | tf_op jit(solution)/shard_map/jit(_take)/gather | solution.py:47
  146.7 2.4 copy.14
  149.1 92.8 %all-gather.3.cloned.1.call-done = bf16[1,2048,512]{1,0,2:T(2,128)(2,1)} async-done(((bf16[1,256,512]{1,0,2:T(2,128)(2,1)}), bf16[1,2048,512]{1,0,2:T(2,128)(2,1)}) %all-gather.3.cloned.1.call-update) | async-done | bytes 2097168 | tf_op jit(solution)/shard_map/all_gather | solution.py:44
  241.9 9.0 %copy.13 = bf16[1,2048,512]{2,1,0:T(8,128)(2,1)S(1)} copy(bf16[1,2048,512]{1,0,2:T(2,128)(2,1)} %all-gather.3.cloned.1.call-done) | data formatting | bytes 4194304 | tf_op jit(solution)/shard_map/all_gather | solution.py:44
  250.9 9.7 %fusion = bf16[2048,512]{0,1:T(8,128)(2,1)} fusion(bf16[2048,2048]{1,0:T(8,128)(2,1)} %param.10, bf16[1,2048,512]{2,1,0:T(8,128)(2,1)S(1)} %copy.13, bf16[2048,512]{0,1:T(8,128)(2,1)} %copy.14, pred[2048]{0:T(1024)(128)(4,1)S(1)} %compare_and_fusion), kind=kOutput, calls=%fused_computation.2 | convolution fusion | flops 4299161600 | bytes 14682112 | tf_op jit(solution)/shard_map/dot_general | solution.py:46
  260.6 3.9 %copy.15 = bf16[2048,512]{1,0:T(8,128)(2,1)} copy(bf16[2048,512]{0,1:T(8,128)(2,1)} %fusion) | data formatting | bytes 4194304 | tf_op jit(solution)/shard_map/convert_element_type | solution.py:48
  (3 shorter events, 0.1 us)
Async XLA Ops:
  6.5 1.0 copy-start
  6.5 235.4 %all-gather.3.cloned.1.call-start = ((), (), s32[]{:S(2)}) async-start(), calls=%async_computation | async-start | bytes 4718592 | tf_op jit(solution)/shard_map/all_gather | solution.py:44
  8.8 30.3 %collective-permute-start = (f32[256,512]{1,0:T(8,128)S(1)}, f32[256,512]{1,0:T(8,128)}, u32[]{:S(2)}, u32[]{:S(2)}) collective-permute-start(f32[256,512]{1,0:T(8,128)S(1)} %fusion.4), channel_id=1, source_target_pairs={} | collective-permute-start | bytes 1572872 | tf_op jit(solution)/shard_map/ppermute | solution.py:10
  10.3 29.9 %collective-permute-start.1 = (f32[256,512]{1,0:T(8,128)S(1)}, f32[256,512]{1,0:T(8,128)}, u32[]{:S(2)}, u32[]{:S(2)}) collective-permute-start(f32[256,512]{1,0:T(8,128)S(1)} %fusion.4), channel_id=1, source_target_pairs={{0,3},{4,7},{8,11},{12,15},{16,19},{20,23},{24,27},{28,31}} | collective-permute-start | bytes 1572872 | tf_op jit(solution)/shard_map/ppermute | solution.py:10
  15.4 25.9 %collective-permute-start.2 = (f32[256,512]{1,0:T(8,128)S(1)}, f32[256,512]{1,0:T(8,128)}, u32[]{:S(2)}, u32[]{:S(2)}) collective-permute-start(f32[256,512]{1,0:T(8,128)S(1)} %fusion.4), channel_id=1, source_target_pairs={{0,2},{1,3},{4,6},{5,7},{8,10},{9,11},{12,14},{13,15},{16,18},{17,... | collective-permute-start | bytes 1572872 | tf_op jit(solution)/shard_map/ppermute | solution.py:10
  17.5 24.9 %collective-permute-start.3 = (f32[256,512]{1,0:T(8,128)S(1)}, f32[256,512]{1,0:T(8,128)}, u32[]{:S(2)}, u32[]{:S(2)}) collective-permute-start(f32[256,512]{1,0:T(8,128)S(1)} %fusion.4), channel_id=1, source_target_pairs={{0,1},{1,2},{2,3},{4,5},{5,6},{6,7},{8,9},{9,10},{10,11},{12,13},{... | collective-permute-start | bytes 1572872 | tf_op jit(solution)/shard_map/ppermute | solution.py:10
  48.3 90.9 %copy-start.1 = (s32[2048]{0:T(1024)S(1)}, s32[2048]{0:T(1024)}, u32[]{:S(2)}) copy-start(s32[2048]{0:T(1024)} %param.11) | copy-start | bytes 24580
Sparse Core Ops, SparseCore 0:
  139.3 102.5 all-gather.2
where the time goes:
time: 272 us; the launch traced here: 271 us
  matrix products  102 us (38%)
  waiting for transfers between devices  92.8 us (34%)
  local copies, waits for them, and re-layouts  50.7 us (19%)
  between operations  13.5 us (5%)
  starting transfers between devices  10.8 us (4%)
    all_gather x1, waiting for transfers between devices, per_device(): lax.all_gather(part, 'mode', axis=0, tiled=True)  92.8 us
    conv_general_dilated x1, matrix products, depthwise(): lax.conv_general_dilated(signal[None], flipped, (1,), 'VALID', dimension_...  90.9 us
    rev x1, local copies, waits for them, and re-layouts, depthwise(): flipped = jnp.flip(weights, 1)[:, None, :]  11.6 us
    ppermute x4, starting transfers between devices, passed_along(): return lax.ppermute(block, axis, route)  10.7 us
    gather x2, local copies, waits for them, and re-layouts, per_device(): ground = jnp.take(support_accel, groups, axis=0).astype(jnp.float32)  9.92 us
    dot_general x1, matrix products, per_device(): jnp.dot(columns, piece, preferred_element_type=jnp.float32)  9.71 us
    all_gather x1, local copies, waits for them, and re-layouts, per_device(): lax.all_gather(part, 'mode', axis=0, tiled=True)  8.97 us
    broadcast_in_dim x1, local copies, waits for them, and re-layouts, depthwise(): flipped = jnp.flip(weights, 1)[:, None, :]  6.06 us
  transfers between devices with their start and end apart: 5, of which 1 were waited for; matrix products, arithmetic and copies ran while one was open for 12% of the time, Pallas kernels for 0%

commit v1 on v0

--- a/solution.py
+++ b/solution.py
@@ -2,6 +2,27 @@
 import jax.numpy as jnp
 from jax import lax
 from jax.sharding import PartitionSpec as P
+
+
+def gather_around(array, axis, dim):
+    devices, index, rows = (lax.axis_size(axis), lax.axis_index(axis), array.shape[dim])
+    ahead = [(i, (i + 1) % devices) for i in range(devices)]
+    behind = [(i, (i - 1) % devices) for i in range(devices)]
+    filled = jnp.zeros((*array.shape[:dim], devices * rows, *array.shape[dim + 1 :]), array.dtype)
+    filled = lax.dynamic_update_slice_in_dim(filled, array, index * rows, axis=dim)
+    from_left = from_right = array
+    middle = devices // 2
+    for lap in range(1, middle + 1):
+        from_left = lax.ppermute(from_left, axis, ahead)
+        filled = lax.dynamic_update_slice_in_dim(
+            filled, from_left, (index - lap) % devices * rows, axis=dim
+        )
+        if lap < devices - middle:
+            from_right = lax.ppermute(from_right, axis, behind)
+            filled = lax.dynamic_update_slice_in_dim(
+                filled, from_right, (index + lap) % devices * rows, axis=dim
+            )
+    return filled
 
 
 def passed_along(block, axis, distance):
@@ -41,7 +62,7 @@
     window = jnp.concatenate(pieces, axis=1)
     modal = apply_filter(window[:, 1:], masked).astype(jnp.bfloat16)
     initial = jnp.zeros((mode_shapes.shape[0], slab_len), jnp.float32)
-    piece = jax.tree.map(lambda part: lax.all_gather(part, "mode", axis=0, tiled=True), modal)
+    piece = jax.tree.map(lambda part: gather_around(part, "mode", 0), modal)
     columns = lax.slice_in_dim(mode_shapes, 0, piece.shape[0], axis=1)
     summed = initial + jnp.dot(columns, piece, preferred_element_type=jnp.float32)
     ground = jnp.take(support_accel, groups, axis=0).astype(jnp.float32)

time: 272 us -> 191 us (0.70)
  waiting for transfers between devices: 92.8 us -> 19.3 us
  starting transfers between devices: 10.8 us -> 28.6 us
  between operations: 13.5 us -> 0.21 us
  local copies, waits for them, and re-layouts: 50.7 us -> 42.4 us
  matrix products: 102 us -> 98.4 us
    all_gather x1 -> x0, waiting for transfers between devices: 92.8 us -> none  [per_device(): lax.all_gather(part, 'mode', axis=0, tiled=True)]
    ppermute x0 -> x7, waiting for transfers between devices: none -> 19.3 us  [the longest x4 12.3 us: gather_around(): from_left = lax.ppermute(from_left, axis, ahead)]
    ppermute x0 -> x7, starting transfers between devices: none -> 17.9 us  [the longest x3 13.6 us: gather_around(): from_right = lax.ppermute(from_right, axis, behind)]
    all_gather x1 -> x0, local copies, waits for them, and re-layouts: 8.97 us -> none  [per_device(): lax.all_gather(part, 'mode', axis=0, tiled=True)]
  transfers between devices with their start and end apart: 5 -> 11, of which waited for: 1 -> 4; matrix products, arithmetic and copies ran while one was open for 12% -> 18% of each run, Pallas kernels for 0% -> 0%
where the time goes in v1:
time: 191 us
  matrix products  98.4 us (52%)
  local copies, waits for them, and re-layouts  42.4 us (22%)
  starting transfers between devices  28.6 us (15%)
  waiting for transfers between devices  19.3 us (10%)
    conv_general_dilated x1, matrix products, depthwise(): lax.conv_general_dilated(signal[None], flipped, (1,), 'VALID', dimension_...  88.7 us
    ppermute x3, starting transfers between devices, gather_around(): from_right = lax.ppermute(from_right, axis, behind)  13.6 us
    ppermute x4, waiting for transfers between devices, gather_around(): from_left = lax.ppermute(from_left, axis, ahead)  12.3 us
    rev x1, local copies, waits for them, and re-layouts, depthwise(): flipped = jnp.flip(weights, 1)[:, None, :]  11.6 us
    ppermute x4, starting transfers between devices, passed_along(): return lax.ppermute(block, axis, route)  10.8 us
    gather x2, local copies, waits for them, and re-layouts, per_device(): ground = jnp.take(support_accel, groups, axis=0).astype(jnp.float32)  9.91 us
    dot_general x1, matrix products, per_device(): jnp.dot(columns, piece, preferred_element_type=jnp.float32)  8.39 us
    ppermute x3, waiting for transfers between devices, gather_around(): from_right = lax.ppermute(from_right, axis, behind)  7.01 us
  transfers between devices with their start and end apart: 11, of which 4 were waited for; matrix products, arithmetic and copies ran while one was open for 18% of the time, Pallas kernels for 0%

profile of v1, /device:TPU:0, one launch (start us, length us, event | category | flops | bytes accessed | tf_op | source)
XLA Modules:
  0.0 190.7 jit_solution(9105364130895350080)
XLA Ops:
  0.0 1.0 copy-done
  1.0 1.2 fusion.3
  2.3 1.5 collective-permute-start
  3.8 5.1 %collective-permute-start.1 = (f32[256,512]{1,0:T(8,128)S(1)}, f32[256,512]{1,0:T(8,128)}, u32[]{:S(2)}, u32[]{:S(2)}) collective-permute-start(f32[256,512]{1,0:T(8,128)S(1)} %fusion.3), channel_id=1, source_target_pairs={{0,3},{4,7},{8,11},{12,15},{16,19},{20,23},{24,27},{28,31}} | collective-permute-start | bytes 1572872 | tf_op jit(solution)/shard_map/ppermute | solution.py:31
  8.9 2.1 %collective-permute-start.2 = (f32[256,512]{1,0:T(8,128)S(1)}, f32[256,512]{1,0:T(8,128)}, u32[]{:S(2)}, u32[]{:S(2)}) collective-permute-start(f32[256,512]{1,0:T(8,128)S(1)} %fusion.3), channel_id=1, source_target_pairs={{0,2},{1,3},{4,6},{5,7},{8,10},{9,11},{12,14},{13,15},{16,18},{17,... | collective-permute-start | bytes 1572872 | tf_op jit(solution)/shard_map/ppermute | solution.py:31
  11.0 2.1 %collective-permute-start.3 = (f32[256,512]{1,0:T(8,128)S(1)}, f32[256,512]{1,0:T(8,128)}, u32[]{:S(2)}, u32[]{:S(2)}) collective-permute-start(f32[256,512]{1,0:T(8,128)S(1)} %fusion.3), channel_id=1, source_target_pairs={{0,1},{1,2},{2,3},{4,5},{5,6},{6,7},{8,9},{9,10},{10,11},{12,13},{... | collective-permute-start | bytes 1572872 | tf_op jit(solution)/shard_map/ppermute | solution.py:31
  13.0 1.8 fusion.1
  14.8 11.6 %rev.4 = f32[256,2048]{1,0:T(8,128)} reverse(f32[256,2048]{1,0:T(8,128)S(1)} %fusion.1), dimensions={1} | reverse | bytes 4194304 | tf_op jit(solution)/shard_map/jit(_flip)/rev | solution.py:35
  26.5 6.1 %copy.12 = f32[256,1,2048]{0,1,2:T(1,128)} copy(f32[256,1,2048]{2,0,1:T(8,128)} %bitcast.15) | data formatting | bytes 4194304 | tf_op jit(solution)/shard_map/broadcast_in_dim | solution.py:35
  32.6 1.1 constant_dynamic-update-slice_fusion.4
  33.6 1.1 constant_dynamic-update-slice_fusion.3
  34.7 1.1 constant_dynamic-update-slice_fusion.2
  35.8 1.1 constant_dynamic-update-slice_fusion.1
  37.0 0.8 slice_bitcast_fusion
  37.7 4.0 %copy.11 = f32[1,256,2559]{1,0,2:T(1,128)} copy(f32[1,256,2559]{2,1,0:T(8,128)S(1)} %slice_bitcast_fusion) | data formatting | bytes 5240832 | tf_op jit(solution)/shard_map/broadcast_in_dim | solution.py:37
  41.7 88.7 %convolution_convert_fusion = bf16[1,256,512]{1,0,2:T(2,128)(2,1)S(1)} fusion(f32[1,256,2559]{1,0,2:T(1,128)} %copy.11, f32[256,1,2048]{0,1,2:T(1,128)} %copy.12), kind=kOutput, calls=%fused_computation.6 | convolution fusion | flops 3221356544 | bytes 4979712 | tf_op jit(solution)/shard_map/conv_general_dilated | solution.py:36
  130.5 0.7 copy.13
  131.2 1.6 collective-permute-start.4
  132.7 3.2 %collective-permute-start.5 = (bf16[256,512]{1,0:T(8,128)(2,1)S(1)}, bf16[256,512]{1,0:T(8,128)(2,1)S(1)}, u32[]{:S(2)}, u32[]{:S(2)}) collective-permute-start(bf16[256,512]{1,0:T(8,128)(2,1)S(1)} %bitcast.17), channel_id=1, source_target_pairs={{0,28},{4,0},{8,4},{12,8},{16,12},{20,16},{24,20},{28,24},{1,29},{... | collective-permute-start | bytes 786440 | tf_op jit(solution)/shard_map/ppermute | solution.py:21
  135.9 7.3 %collective-permute-done.4 = bf16[256,512]{1,0:T(8,128)(2,1)} collective-permute-done((bf16[256,512]{1,0:T(8,128)(2,1)S(1)}, bf16[256,512]{1,0:T(8,128)(2,1)}, u32[]{:S(2)}, u32[]{:S(2)}) %collective-permute-start.4) | collective-permute-done | bytes 262176 | tf_op jit(solution)/shard_map/ppermute | solution.py:16
  143.2 2.6 %collective-permute-start.6 = (bf16[256,512]{1,0:T(8,128)(2,1)}, bf16[256,512]{1,0:T(8,128)(2,1)S(1)}, u32[]{:S(2)}, u32[]{:S(2)}) collective-permute-start(bf16[256,512]{1,0:T(8,128)(2,1)} %collective-permute-done.4), channel_id=1, source_target_pairs={{0,4},{4,8},{8,12},{12,16},{16,20},{20,24},{24,28},{28,0},{1,5},{5... | collective-permute-start | bytes 786440 | tf_op jit(solution)/shard_map/ppermute | solution.py:16
  145.8 7.5 %gather_fusion = bf16[2048,512]{1,0:T(8,128)(2,1)S(1)} fusion(bf16[512,512]{1,0:T(8,128)(2,1)S(1)} %copy-done, s32[2048]{0:T(1024)S(1)} %fusion.2), kind=kCustom, calls=%fused_computation | custom fusion | bytes 4202496 | tf_op jit(solution)/shard_map/jit(_take)/gather | solution.py:68
  153.4 2.4 %copy.14 = bf16[2048,512]{0,1:T(8,128)(2,1)} copy(bf16[2048,512]{1,0:T(8,128)(2,1)S(1)} %gather_fusion) | data formatting | bytes 4194304 | tf_op jit(solution)/shard_map/jit(_take)/gather | solution.py:68
  155.8 3.2 %collective-permute-start.7 = (bf16[256,512]{1,0:T(8,128)(2,1)S(1)}, bf16[256,512]{1,0:T(8,128)(2,1)S(1)}, u32[]{:S(2)}, u32[]{:S(2)}) collective-permute-start(bf16[256,512]{1,0:T(8,128)(2,1)S(1)} %collective-permute-done.5), channel_id=1, source_target_pairs={{0,28},{4,0},{8,4},{12,8},{16,12},{20,16},{24,20},{28,24},{1,29},{... | collective-permute-start | bytes 786440 | tf_op jit(solution)/shard_map/ppermute | solution.py:21
  158.9 0.1 broadcast_in_dim.26
  159.2 1.1 constant_dynamic-update-slice_fusion.11
  160.3 2.6 %collective-permute-done.7 = bf16[256,512]{1,0:T(8,128)(2,1)S(1)} collective-permute-done((bf16[256,512]{1,0:T(8,128)(2,1)S(1)}, bf16[256,512]{1,0:T(8,128)(2,1)S(1)}, u32[]{:S(2)}, u32[]{:S(2)}) %collective-permute-start.7) | collective-permute-done | bytes 262176 | tf_op jit(solution)/shard_map/ppermute | solution.py:21
  163.0 7.2 %collective-permute-start.9 = (bf16[256,512]{1,0:T(8,128)(2,1)S(1)}, bf16[256,512]{1,0:T(8,128)(2,1)S(1)}, u32[]{:S(2)}, u32[]{:S(2)}) collective-permute-start(bf16[256,512]{1,0:T(8,128)(2,1)S(1)} %collective-permute-done.7), channel_id=1, source_target_pairs={{0,28},{4,0},{8,4},{12,8},{16,12},{20,16},{24,20},{28,24},{1,29},{... | collective-permute-start | bytes 786440 | tf_op jit(solution)/shard_map/ppermute | solution.py:21
  170.4 4.4 %collective-permute-done.9 = bf16[256,512]{1,0:T(8,128)(2,1)S(1)} collective-permute-done((bf16[256,512]{1,0:T(8,128)(2,1)S(1)}, bf16[256,512]{1,0:T(8,128)(2,1)S(1)}, u32[]{:S(2)}, u32[]{:S(2)}) %collective-permute-start.9) | collective-permute-done | bytes 262176 | tf_op jit(solution)/shard_map/ppermute | solution.py:21
  174.8 5.0 %collective-permute-done.10 = bf16[256,512]{1,0:T(8,128)(2,1)S(1)} collective-permute-done((bf16[256,512]{1,0:T(8,128)(2,1)S(1)}, bf16[256,512]{1,0:T(8,128)(2,1)S(1)}, u32[]{:S(2)}, u32[]{:S(2)}) %collective-permute-start.10) | collective-permute-done | bytes 262176 | tf_op jit(solution)/shard_map/ppermute | solution.py:16
  179.8 8.4 %fusion = bf16[2048,512]{0,1:T(8,128)(2,1)S(1)} fusion(bf16[2048,512]{1,0:T(8,128)(2,1)S(1)} %constant_dynamic-update-slice_fusion.5, bf16[2048,2048]{1,0:T(8,128)(2,1)} %param.10, bf16[2048,512]{0,1:T(8,128)(2,1)S(1)} %copy-done.1, pred[2048]{0:T(1024)(128)(4,1)S(1)} %compare_and_fusion), kind=kOutput, calls=%fused_computation.2 | convolution fusion | flops 4299161600 | bytes 14682112 | tf_op jit(solution)/shard_map/dot_general | solution.py:67
  188.2 2.5 %copy.15 = bf16[2048,512]{1,0:T(8,128)(2,1)} copy(bf16[2048,512]{0,1:T(8,128)(2,1)S(1)} %fusion) | data formatting | bytes 4194304 | tf_op jit(solution)/shard_map/convert_element_type | solution.py:69
  (24 shorter events, 0.4 us)
Async XLA Ops:
  0.0 1.0 copy-start
  2.3 30.3 %collective-permute-start = (f32[256,512]{1,0:T(8,128)S(1)}, f32[256,512]{1,0:T(8,128)}, u32[]{:S(2)}, u32[]{:S(2)}) collective-permute-start(f32[256,512]{1,0:T(8,128)S(1)} %fusion.3), channel_id=1, source_target_pairs={} | collective-permute-start | bytes 1572872 | tf_op jit(solution)/shard_map/ppermute | solution.py:31
  3.8 29.9 %collective-permute-start.1 = (f32[256,512]{1,0:T(8,128)S(1)}, f32[256,512]{1,0:T(8,128)}, u32[]{:S(2)}, u32[]{:S(2)}) collective-permute-start(f32[256,512]{1,0:T(8,128)S(1)} %fusion.3), channel_id=1, source_target_pairs={{0,3},{4,7},{8,11},{12,15},{16,19},{20,23},{24,27},{28,31}} | collective-permute-start | bytes 1572872 | tf_op jit(solution)/shard_map/ppermute | solution.py:31
  8.9 25.9 %collective-permute-start.2 = (f32[256,512]{1,0:T(8,128)S(1)}, f32[256,512]{1,0:T(8,128)}, u32[]{:S(2)}, u32[]{:S(2)}) collective-permute-start(f32[256,512]{1,0:T(8,128)S(1)} %fusion.3), channel_id=1, source_target_pairs={{0,2},{1,3},{4,6},{5,7},{8,10},{9,11},{12,14},{13,15},{16,18},{17,... | collective-permute-start | bytes 1572872 | tf_op jit(solution)/shard_map/ppermute | solution.py:31
  11.0 24.8 %collective-permute-start.3 = (f32[256,512]{1,0:T(8,128)S(1)}, f32[256,512]{1,0:T(8,128)}, u32[]{:S(2)}, u32[]{:S(2)}) collective-permute-start(f32[256,512]{1,0:T(8,128)S(1)} %fusion.3), channel_id=1, source_target_pairs={{0,1},{1,2},{2,3},{4,5},{5,6},{6,7},{8,9},{9,10},{10,11},{12,13},{... | collective-permute-start | bytes 1572872 | tf_op jit(solution)/shard_map/ppermute | solution.py:31
  41.7 94.2 %copy-start.2 = (s32[2048]{0:T(1024)S(1)}, s32[2048]{0:T(1024)}, u32[]{:S(2)}) copy-start(s32[2048]{0:T(1024)} %param.11) | copy-start | bytes 24580
  131.2 12.1 %collective-permute-start.4 = (bf16[256,512]{1,0:T(8,128)(2,1)S(1)}, bf16[256,512]{1,0:T(8,128)(2,1)}, u32[]{:S(2)}, u32[]{:S(2)}) collective-permute-start(bf16[256,512]{1,0:T(8,128)(2,1)S(1)} %bitcast.16), channel_id=1, source_target_pairs={{0,4},{4,8},{8,12},{12,16},{16,20},{20,24},{24,28},{28,0},{1,5},{5... | collective-permute-start | bytes 786440 | tf_op jit(solution)/shard_map/ppermute | solution.py:16
  132.7 23.0 %collective-permute-start.5 = (bf16[256,512]{1,0:T(8,128)(2,1)S(1)}, bf16[256,512]{1,0:T(8,128)(2,1)S(1)}, u32[]{:S(2)}, u32[]{:S(2)}) collective-permute-start(bf16[256,512]{1,0:T(8,128)(2,1)S(1)} %bitcast.17), channel_id=1, source_target_pairs={{0,28},{4,0},{8,4},{12,8},{16,12},{20,16},{24,20},{28,24},{1,29},{... | collective-permute-start | bytes 786440 | tf_op jit(solution)/shard_map/ppermute | solution.py:21
  143.2 15.9 %collective-permute-start.6 = (bf16[256,512]{1,0:T(8,128)(2,1)}, bf16[256,512]{1,0:T(8,128)(2,1)S(1)}, u32[]{:S(2)}, u32[]{:S(2)}) collective-permute-start(bf16[256,512]{1,0:T(8,128)(2,1)} %collective-permute-done.4), channel_id=1, source_target_pairs={{0,4},{4,8},{8,12},{12,16},{16,20},{20,24},{24,28},{28,0},{1,5},{5... | collective-permute-start | bytes 786440 | tf_op jit(solution)/shard_map/ppermute | solution.py:16
  155.8 7.2 %collective-permute-start.7 = (bf16[256,512]{1,0:T(8,128)(2,1)S(1)}, bf16[256,512]{1,0:T(8,128)(2,1)S(1)}, u32[]{:S(2)}, u32[]{:S(2)}) collective-permute-start(bf16[256,512]{1,0:T(8,128)(2,1)S(1)} %collective-permute-done.5), channel_id=1, source_target_pairs={{0,28},{4,0},{8,4},{12,8},{16,12},{20,16},{24,20},{28,24},{1,29},{... | collective-permute-start | bytes 786440 | tf_op jit(solution)/shard_map/ppermute | solution.py:21
  159.1 20.7 %copy-start.1 = (bf16[2048,512]{0,1:T(8,128)(2,1)S(1)}, bf16[2048,512]{0,1:T(8,128)(2,1)}, u32[]{:S(2)}) copy-start(bf16[2048,512]{0,1:T(8,128)(2,1)} %copy.14) | copy-start | bytes 6291460
  159.1 11.1 %collective-permute-start.8 = (bf16[256,512]{1,0:T(8,128)(2,1)S(1)}, bf16[256,512]{1,0:T(8,128)(2,1)S(1)}, u32[]{:S(2)}, u32[]{:S(2)}) collective-permute-start(bf16[256,512]{1,0:T(8,128)(2,1)S(1)} %collective-permute-done.6), channel_id=1, source_target_pairs={{0,4},{4,8},{8,12},{12,16},{16,20},{20,24},{24,28},{28,0},{1,5},{5... | collective-permute-start | bytes 786440 | tf_op jit(solution)/shard_map/ppermute | solution.py:16
  163.0 11.8 %collective-permute-start.9 = (bf16[256,512]{1,0:T(8,128)(2,1)S(1)}, bf16[256,512]{1,0:T(8,128)(2,1)S(1)}, u32[]{:S(2)}, u32[]{:S(2)}) collective-permute-start(bf16[256,512]{1,0:T(8,128)(2,1)S(1)} %collective-permute-done.7), channel_id=1, source_target_pairs={{0,28},{4,0},{8,4},{12,8},{16,12},{20,16},{24,20},{28,24},{1,29},{... | collective-permute-start | bytes 786440 | tf_op jit(solution)/shard_map/ppermute | solution.py:21
  170.2 9.5 %collective-permute-start.10 = (bf16[256,512]{1,0:T(8,128)(2,1)S(1)}, bf16[256,512]{1,0:T(8,128)(2,1)S(1)}, u32[]{:S(2)}, u32[]{:S(2)}) collective-permute-start(bf16[256,512]{1,0:T(8,128)(2,1)S(1)} %collective-permute-done.8), channel_id=1, source_target_pairs={{0,4},{4,8},{8,12},{12,16},{16,20},{20,24},{24,28},{28,0},{1,5},{5... | collective-permute-start | bytes 786440 | tf_op jit(solution)/shard_map/ppermute | solution.py:16
